TPU v7x, 32 devices: a whole 2x2x4 slice. The times are simulated.
32 devices in a mesh: grp: 2 (over x), bits: 16 (over z, y, core).
Axes of the slice: x: 2, y: 2, z: 4, core: 2. Of those that a mesh axis runs over, the one named last changes fastest.
Arguments:
- prefix: bfloat16 [128, 16, 1024], P(('grp', 'bits')), parts along dimension 0, may hold values from -6 to 6
- first_suffix: bfloat16 [8, 2, 512, 512], P('grp', None, 'bits'), parts along dimension 0, may hold values from -0.109375 to 0.109375
- pair_prefix: int32 [256, 3], P(('grp', 'bits')), parts along dimension 0, may hold values from 0 to 3
- pair_suffix: int32 [256, 3], P(('grp', 'bits')), parts along dimension 0, may hold values from 0 to 3, all different within a row
- merge_count: int32 [256], P(('grp', 'bits')), parts along dimension 0, may hold values from 1 to 3, as said below
- suffix: bfloat16 [32, 2, 512, 512], P(('grp', 'bits')), parts along dimension 0, may hold values from -0.1875 to 0.1875
- routes: int32 [256, 12], P(('grp', 'bits')), parts along dimension 0, may hold values from 0 to 15, all different within a row; in each aligned block of 8 rows (0 to 7, 8 to 15, ...) at most 8 rows name the same one
- cap: bfloat16 [2, 512, 64], replicated, may hold values from -0.0546875 to 0.0546875
Outputs:
- capped: float32 [256, 16, 128], P(('grp', 'bits')), parts along dimension 0
There are 2 independent parts, one for each index of `grp`. A program takes and returns all parts, laid end to end along the dimension named above; an argument that names none is the same for every part. Nothing has to cross between parts.
Inputs may be any that keep to these rules, and one draw needn't show every extreme that they name: `pair_suffix`: each row names 3 different lifetime-one blocks. `merge_count`: some piece has exactly 3 merges and some exactly one. `routes`: each row names 12 different suffixes; in each aligned block of 8 rows no suffix is named by more than 8 rows, a bound that some block reaches.
All inputs are finite; a program needn't handle non-finite values.
Results may differ from a plain program's by a relative error of at most 0.005.
Values may be sent and summed in bfloat16 or wider, within the bound.
A program may use at most 64 MiB of HBM per device.

v0:
```python
import jax
import jax.numpy as jnp
from jax import lax
from jax.sharding import PartitionSpec as P

HIGHEST_PRECISION = lax.Precision.HIGHEST


def complex_form(blocks):
    real_part = blocks[..., 0, :, :]
    imag_part = blocks[..., 1, :, :]
    upper_half = jnp.concatenate([real_part, imag_part], axis=-1)
    lower_half = jnp.concatenate([-imag_part, real_part], axis=-1)
    return jnp.concatenate([upper_half, lower_half], axis=-2)


def on_device(prefix, first_suffix, pair_prefix, pair_suffix, merge_count, suffix, routes, cap):
    pieces = pair_prefix.shape[0]
    merges = pair_prefix.shape[1]
    held_blocks = prefix.shape[0]
    rows_piece = prefix.shape[1]
    twice_width = prefix.shape[2]
    half_width = twice_width // 2
    first_count = first_suffix.shape[0]
    listed = routes.shape[1]
    owners = lax.axis_size("bits")
    slot_count = min(pieces, max(2, (2 * pieces * listed + owners - 1) // owners))
    live_mask = lax.broadcasted_iota(jnp.int32, (pieces, merges), 1) < merge_count[:, None]
    matches = (
        pair_suffix[:, :, None] == lax.broadcasted_iota(jnp.int32, (pieces, merges, first_count), 2)
    ) & live_mask[:, :, None]
    which_block = pair_prefix[:, :, None] == lax.broadcasted_iota(
        jnp.int32, (pieces, merges, held_blocks), 2
    )
    prefix_picks = jnp.einsum(
        "ika,ikp->iap", matches.astype(jnp.float32), which_block.astype(jnp.float32)
    ).astype(jnp.bfloat16)
    selected = jnp.einsum(
        "iap,prc->airc", prefix_picks, prefix, preferred_element_type=jnp.float32
    ).astype(jnp.bfloat16)
    selected = selected.reshape(first_count, pieces * rows_piece, twice_width)
    portion = lax.all_gather(first_suffix, "bits", axis=2, tiled=True)
    count_rows = portion.shape[2]
    real_cols = lax.slice_in_dim(selected, 0, count_rows, axis=2)
    imag_cols = lax.dynamic_slice_in_dim(selected, half_width, count_rows, 2)
    left_side = jnp.concatenate([real_cols, imag_cols], axis=2)
    upper_half = jnp.concatenate([portion[:, 0], portion[:, 1]], axis=2)
    lower_half = jnp.concatenate([-portion[:, 1], portion[:, 0]], axis=2)
    right_side = jnp.concatenate([upper_half, lower_half], axis=1)
    state_rows = jnp.einsum(
        "arc,acw->rw", left_side, right_side, preferred_element_type=jnp.float32
    )
    state_rows = state_rows.astype(jnp.bfloat16).reshape(pieces, rows_piece, twice_width)
    named_by = jnp.sum(
        (routes[:, :, None] == lax.broadcasted_iota(jnp.int32, (pieces, listed, owners), 2)).astype(
            jnp.int32
        ),
        axis=1,
    )
    slot_rank = jnp.cumsum(named_by, axis=0) - named_by
    slot_hit = (
        slot_rank[:, :, None] == lax.broadcasted_iota(jnp.int32, (pieces, owners, slot_count), 2)
    ) & (named_by[:, :, None] > 0)
    dispatch = jnp.transpose(slot_hit, (1, 2, 0)).astype(jnp.bfloat16)
    outgoing = jnp.einsum(
        "dmi,irc->dmrc", dispatch, state_rows, preferred_element_type=jnp.float32
    ).astype(jnp.bfloat16)
    own_form = complex_form(suffix[0])
    cap_form = complex_form(cap)
    products = jnp.einsum(
        "smrc,cw->smrw",
        lax.all_to_all(outgoing, "bits", split_axis=0, concat_axis=0, tiled=True),
        own_form,
        preferred_element_type=jnp.float32,
    ).astype(jnp.bfloat16)
    capped_terms = jnp.einsum(
        "smrw,wv->smrv", products, cap_form, preferred_element_type=jnp.float32
    )
    returned = lax.all_to_all(
        capped_terms.astype(jnp.bfloat16), "bits", split_axis=0, concat_axis=0, tiled=True
    ).astype(capped_terms.dtype)
    return jnp.einsum(
        "dmi,dmrv->irv", dispatch.astype(jnp.float32), returned, precision=HIGHEST_PRECISION
    )


def solution(mesh):
    return jax.shard_map(
        on_device,
        mesh=mesh,
        in_specs=(
            P(("grp", "bits"), None, None),
            P("grp", None, "bits", None),
            P(("grp", "bits"), None),
            P(("grp", "bits"), None),
            P(("grp", "bits")),
            P(("grp", "bits"), None, None, None),
            P(("grp", "bits"), None),
            P(),
        ),
        out_specs=P(("grp", "bits"), None, None),
        check_vma=False,
    )
```

profile of v0, /device:TPU:0, one launch (start us, length us, event | category | flops | bytes accessed | tf_op | source)
XLA Modules:
  0.0 205.2 jit_solution(14975206516049845053)
XLA Ops:
  6.5 0.0 all-gather.2.cloned.1.call-start
  6.5 1.7 copy.52
  8.2 0.0 all-gather.2.cloned.1.call-update
  8.2 0.8 copy.47
  9.0 0.8 copy.48
  9.7 0.7 iota_compare_fusion.5
  10.5 0.2 fusion.32
  10.7 1.3 fusion.22
  12.0 0.6 copy.51
  12.6 0.8 copy.46
  13.3 0.1 convert_reduce_fusion
  13.5 49.2 %all-gather.2.cloned.1.call-done = bf16[4,2,512,512]{3,2,0,1:T(8,128)(2,1)} async-done(((bf16[4,2,32,512]{3,2,0,1:T(8,128)(2,1)}), bf16[4,2,512,512]{3,2,0,1:T(8,128)(2,1)}) %all-gather.2.cloned.1.call-update) | async-done | bytes 4194320 | tf_op jit(solution)/shard_map/all_gather | solution.py:42
  62.7 0.0 copy-start
  62.7 2.7 %slice_bitcast_fusion = (bf16[4,512,512]{2,1,0:T(8,128)(2,1)S(1)}, bf16[4,512,512]{2,1,0:T(8,128)(2,1)S(1)}) fusion(bf16[4,2,512,512]{3,2,0,1:T(8,128)(2,1)} %all-gather.2.cloned.1.call-done), kind=kLoop, calls=%fused_computation.11 | loop fusion | bytes 8388608 | tf_op jit(solution)/shard_map/squeeze | solution.py:47
  65.3 0.8 copy-done
  66.1 0.1 fusion.63
  66.3 1.3 fusion.29
  67.6 1.6 convolution_convert_fusion
  69.1 4.3 %copy.54 = bf16[16,8,16,1024]{3,2,1,0:T(8,128)(2,1)} copy(bf16[16,8,16,1024]{3,0,2,1:T(8,128)(2,1)S(1)} %convolution_convert_fusion) | data formatting | bytes 8388608 | tf_op jit(solution)/shard_map/convert_element_type | solution.py:67
  73.4 0.0 copy-start.2
  73.4 0.0 copy-start.1
  73.4 4.9 %all-to-all-start = ((bf16[16,8,16,1024]{3,2,1,0:T(8,128)(2,1)}), bf16[16,8,16,1024]{3,2,1,0:T(8,128)(2,1)}, u32[]{:S(2)}, u32[]{:S(2)}) async-start(bf16[16,8,16,1024]{3,2,1,0:T(8,128)(2,1)} %copy.54), calls=%async_computation | async-start | bytes 8388608 | tf_op jit(solution)/shard_map/all_to_all | solution.py:72
  78.3 0.0 copy-done.2
  78.3 0.1 copy.68
  78.5 0.1 copy.67
  78.6 0.0 copy-done.1
  78.7 0.1 slice_bitcast_fusion.2
  78.7 76.9 %all-to-all-done = bf16[16,8,16,1024]{3,2,1,0:T(8,128)(2,1)} async-done(((bf16[16,8,16,1024]{3,2,1,0:T(8,128)(2,1)}), bf16[16,8,16,1024]{3,2,1,0:T(8,128)(2,1)}, u32[]{:S(2)}, u32[]{:S(2)}) %all-to-all-start) | async-done | bytes 4194336 | tf_op jit(solution)/shard_map/all_to_all | solution.py:72
  155.6 7.9 %fusion.23 = bf16[16,8,16,128]{3,2,1,0:T(8,128)(2,1)S(1)} fusion(bf16[16,8,16,1024]{3,2,1,0:T(8,128)(2,1)} %all-to-all-done, bf16[512,512]{1,0:T(8,128)(2,1)S(1)} %get-tuple-element.8, bf16[512,512]{1,0:T(8,128)(2,1)S(1)} %fusion.62, bf16[512,512]{1,0:T(8,128)(2,1)S(1)} %get-tuple-element.7, bf16[512,64]{1,0:T(8,128)(2,1)S(1)} %bitcast.66, ...), kind=kOutput, calls=%fused_computation.23 | convolution fusion | flops 4843634688 | bytes 6488064 | tf_op jit(solution)/shard_map/smrw,wv->smrv/dot_general | solution.py:76
  163.5 0.1 copy.57
  163.7 33.7 %all_to_all.10 = bf16[16,8,16,128]{3,1,2,0:T(8,128)(2,1)S(1)} all-to-all(bf16[16,8,16,128]{3,1,2,0:T(8,128)(2,1)S(1)} %copy.57), channel_id=1, replica_groups=mesh['grp'=2,'bits'=16] {'bits'}, dimensions={0} | all-to-all | bytes 1048576 | tf_op jit(solution)/shard_map/all_to_all | solution.py:79
  197.4 0.4 convolution_bitcast_fusion
  197.8 0.6 copy.59
  (6 shorter events, 0.1 us)
Async XLA Ops:
  6.5 56.1 %all-gather.2.cloned.1.call-start = ((), (), s32[]{:S(2)}) async-start(), calls=%async_computation.2 | async-start | bytes 4456448 | tf_op jit(solution)/shard_map/all_gather | solution.py:42
  62.7 3.4 %copy-start = (bf16[4,2,512,512]{3,2,0,1:T(8,128)(2,1)S(1)}, bf16[4,2,512,512]{3,2,0,1:T(8,128)(2,1)}, u32[]{:S(2)}) copy-start(bf16[4,2,512,512]{3,2,0,1:T(8,128)(2,1)} %all-gather.2.cloned.1.call-done) | copy-start | bytes 12582916
  73.4 4.9 %copy-start.2 = (bf16[2,512,64]{1,2,0:T(8,128)(2,1)S(1)}, bf16[2,512,64]{1,2,0:T(8,128)(2,1)}, u32[]{:S(2)}) copy-start(bf16[2,512,64]{1,2,0:T(8,128)(2,1)} %param.15) | copy-start | bytes 393220
  73.4 5.2 %copy-start.1 = (bf16[1,2,512,512]{3,2,1,0:T(8,128)(2,1)S(1)}, bf16[1,2,512,512]{3,2,1,0:T(8,128)(2,1)}, u32[]{:S(2)}) copy-start(bf16[1,2,512,512]{3,2,1,0:T(8,128)(2,1)} %param.13) | copy-start | bytes 3145732
  73.4 82.2 %all-to-all-start = ((bf16[16,8,16,1024]{3,2,1,0:T(8,128)(2,1)}), bf16[16,8,16,1024]{3,2,1,0:T(8,128)(2,1)}, u32[]{:S(2)}, u32[]{:S(2)}) async-start(bf16[16,8,16,1024]{3,2,1,0:T(8,128)(2,1)} %copy.54), calls=%async_computation | async-start | bytes 8388608 | tf_op jit(solution)/shard_map/all_to_all | solution.py:72
Sparse Core Ops, SparseCore 0:
  9.5 53.1 all-gather.1
where the time goes:
time: 206 us; the launch traced here: 205 us
  waiting for transfers between devices  126 us (61%)
  blocking collectives  33.7 us (16%)
  between operations  13.5 us (7%)
  local copies, waits for them, and re-layouts  13.4 us (7%)
  matrix products  12.7 us (6%)
  starting transfers between devices  4.85 us (2%)
    all_to_all x1, waiting for transfers between devices, on_device(): lax.all_to_all(outgoing, 'bits', split_axis=0, concat_axis=0, tiled=True)  76.9 us
    all_gather x1, waiting for transfers between devices, on_device(): portion = lax.all_gather(first_suffix, 'bits', axis=2, tiled=True)  49.2 us
    all_to_all x1, blocking collectives, on_device(): lax.all_to_all(capped_terms.astype(jnp.bfloat16), 'bits', split_axis=0, c...  33.7 us
    dot_general x1, matrix products, on_device(): jnp.einsum('smrw,wv->smrv', products, cap_form, preferred_element_type=jn...  7.92 us
    unnamed x12, local copies, waits for them, and re-layouts  4.98 us
    all_to_all x1, starting transfers between devices, on_device(): lax.all_to_all(outgoing, 'bits', split_axis=0, concat_axis=0, tiled=True)  4.85 us
    convert_element_type x1, local copies, waits for them, and re-layouts, on_device(): outgoing = jnp.einsum('dmi,irc->dmrc', dispatch, state_rows, preferred_el...  4.3 us
  transfers between devices with their start and end apart: 2, of which 2 were waited for; matrix products, arithmetic and copies ran while one was open for 3% of the time, Pallas kernels for 0%

commit v1 on v0

--- a/solution.py
+++ b/solution.py
@@ -4,6 +4,12 @@
 from jax.sharding import PartitionSpec as P
 
 HIGHEST_PRECISION = lax.Precision.HIGHEST
+
+
+def in_order(blocks, dim):
+    shape = list(blocks.shape[1:])
+    shape[dim] *= blocks.shape[0]
+    return jnp.moveaxis(blocks, 0, dim).reshape(shape)
 
 
 def complex_form(blocks):
@@ -39,7 +45,19 @@
         "iap,prc->airc", prefix_picks, prefix, preferred_element_type=jnp.float32
     ).astype(jnp.bfloat16)
     selected = selected.reshape(first_count, pieces * rows_piece, twice_width)
-    portion = lax.all_gather(first_suffix, "bits", axis=2, tiled=True)
+    size = lax.axis_size("bits")
+    pairs = [(i, (i + 1) % size) for i in range(size)]
+    back = [(b, a) for a, b in pairs]
+    lower, upper = ([], [])
+    for step in range(size - 1):
+        if step % 2 == 0:
+            lower.append(lax.ppermute(lower[-1] if lower else first_suffix, "bits", pairs))
+        else:
+            upper.append(lax.ppermute(upper[-1] if upper else first_suffix, "bits", back))
+    blocks_2 = jnp.stack([*lower[::-1], first_suffix, *upper])
+    shift = lax.axis_index("bits") - len(lower)
+    blocks_2 = blocks_2[(jnp.arange(size) - shift) % size]
+    portion = in_order(blocks_2, 2)
     count_rows = portion.shape[2]
     real_cols = lax.slice_in_dim(selected, 0, count_rows, axis=2)
     imag_cols = lax.dynamic_slice_in_dim(selected, half_width, count_rows, 2)

time: 206 us -> 228 us (1.11)
  starting transfers between devices: 4.85 us -> 37.5 us
  local copies, waits for them, and re-layouts: 13.4 us -> 33.5 us
  waiting for transfers between devices: 126 us -> 109 us
  between operations: 13.5 us -> 0.19 us
    all_gather x1 -> x0, waiting for transfers between devices: 49.2 us -> none  [on_device(): portion = lax.all_gather(first_suffix, 'bits', axis=2, tiled=True)]
    ppermute x0 -> x15, starting transfers between devices: none -> 32.6 us  [the longest x7 32.1 us: on_device(): lax.ppermute(upper[-1] if upper else first_suffix, 'bits', back)]
    ppermute x0 -> x15, waiting for transfers between devices: none -> 32.1 us  [the longest x8 27.7 us: on_device(): lax.ppermute(lower[-1] if lower else first_suffix, 'bits', pairs)]
    unnamed x12 -> x30, local copies, waits for them, and re-layouts: 4.98 us -> 19.1 us
    gather x0 -> x1, local copies, waits for them, and re-layouts: none -> 4.99 us  [on_device(): blocks_2 = blocks_2[(jnp.arange(size) - shift) % size]]
    transpose x0 -> x1, local copies, waits for them, and re-layouts: none -> 2.66 us  [in_order(): return jnp.moveaxis(blocks, 0, dim).reshape(shape)]
    squeeze x1, local copies, waits for them, and re-layouts: 2.65 us -> 0.27 us  [on_device(): upper_half = jnp.concatenate([portion[:, 0], portion[:, 1]], axis=2)]
  transfers between devices with their start and end apart: 2 -> 16, of which waited for: 2 -> 13; matrix products, arithmetic and copies ran while one was open for 3% -> 10% of each run, Pallas kernels for 0% -> 0%
where the time goes in v1:
time: 228 us
  waiting for transfers between devices  109 us (48%)
  starting transfers between devices  37.5 us (16%)
  blocking collectives  33.7 us (15%)
  local copies, waits for them, and re-layouts  33.5 us (15%)
  matrix products  12.7 us (6%)
    all_to_all x1, waiting for transfers between devices, on_device(): lax.all_to_all(outgoing, 'bits', split_axis=0, concat_axis=0, tiled=True)  76.9 us
    all_to_all x1, blocking collectives, on_device(): lax.all_to_all(capped_terms.astype(jnp.bfloat16), 'bits', split_axis=0, c...  33.7 us
    ppermute x7, starting transfers between devices, on_device(): lax.ppermute(upper[-1] if upper else first_suffix, 'bits', back)  32.1 us
    ppermute x8, waiting for transfers between devices, on_device(): lax.ppermute(lower[-1] if lower else first_suffix, 'bits', pairs)  27.7 us
    unnamed x30, local copies, waits for them, and re-layouts  19.1 us
    dot_general x1, matrix products, on_device(): jnp.einsum('smrw,wv->smrv', products, cap_form, preferred_element_type=jn...  7.92 us
    gather x1, local copies, waits for them, and re-layouts, on_device(): blocks_2 = blocks_2[(jnp.arange(size) - shift) % size]  4.99 us
    all_to_all x1, starting transfers between devices, on_device(): lax.all_to_all(outgoing, 'bits', split_axis=0, concat_axis=0, tiled=True)  4.84 us
  transfers between devices with their start and end apart: 16, of which 13 were waited for; matrix products, arithmetic and copies ran while one was open for 10% of the time, Pallas kernels for 0%

profile of v1, /device:TPU:0, one launch (start us, length us, event | category | flops | bytes accessed | tf_op | source)
XLA Modules:
  0.0 227.6 jit_solution(16726823598896323727)
XLA Ops:
  0.0 0.5 collective-permute-start
  0.5 9.3 %collective-permute-done = bf16[4,2,32,512]{3,2,1,0:T(8,128)(2,1)S(1)} collective-permute-done((bf16[4,2,32,512]{3,2,1,0:T(8,128)(2,1)}, bf16[4,2,32,512]{3,2,1,0:T(8,128)(2,1)S(1)}, u32[]{:S(2)}, u32[]{:S(2)}) %collective-permute-start) | collective-permute-done | bytes 262176 | tf_op jit(solution)/shard_map/ppermute | solution.py:54
  9.8 0.0 collective-permute-start.1
  9.8 4.4 %collective-permute-start.8 = (bf16[4,2,32,512]{3,2,1,0:T(8,128)(2,1)}, bf16[4,2,32,512]{3,2,1,0:T(8,128)(2,1)S(1)}, u32[]{:S(2)}, u32[]{:S(2)}) collective-permute-start(bf16[4,2,32,512]{3,2,1,0:T(8,128)(2,1)} %param.9), channel_id=1, source_target_pairs={{1,0},{2,1},{3,2},{4,3},{5,4},{6,5},{7,6},{8,7},{9,8},{10,9},{11,1... | collective-permute-start | bytes 786440 | tf_op jit(solution)/shard_map/ppermute | solution.py:56
  14.3 4.1 %collective-permute-done.1 = bf16[4,2,32,512]{3,2,1,0:T(8,128)(2,1)S(1)} collective-permute-done((bf16[4,2,32,512]{3,2,1,0:T(8,128)(2,1)S(1)}, bf16[4,2,32,512]{3,2,1,0:T(8,128)(2,1)S(1)}, u32[]{:S(2)}, u32[]{:S(2)}) %collective-permute-start.1) | collective-permute-done | bytes 262176 | tf_op jit(solution)/shard_map/ppermute | solution.py:54
  18.3 0.2 collective-permute-done.8
  18.5 4.6 %collective-permute-start.9 = (bf16[4,2,32,512]{3,2,1,0:T(8,128)(2,1)S(1)}, bf16[4,2,32,512]{3,2,1,0:T(8,128)(2,1)S(1)}, u32[]{:S(2)}, u32[]{:S(2)}) collective-permute-start(bf16[4,2,32,512]{3,2,1,0:T(8,128)(2,1)S(1)} %collective-permute-done.8), channel_id=1, source_target_pairs={{1,0},{2,1},{3,2},{4,3},{5,4},{6,5},{7,6},{8,7},{9,8},{10,9},{11,1... | collective-permute-start | bytes 786440 | tf_op jit(solution)/shard_map/ppermute | solution.py:56
  23.1 3.8 %collective-permute-done.2 = bf16[4,2,32,512]{3,2,1,0:T(8,128)(2,1)S(1)} collective-permute-done((bf16[4,2,32,512]{3,2,1,0:T(8,128)(2,1)S(1)}, bf16[4,2,32,512]{3,2,1,0:T(8,128)(2,1)S(1)}, u32[]{:S(2)}, u32[]{:S(2)}) %collective-permute-start.2) | collective-permute-done | bytes 262176 | tf_op jit(solution)/shard_map/ppermute | solution.py:54
  26.9 0.0 collective-permute-start.3
  26.9 0.8 copy.46
  27.7 0.0 collective-permute-done.9
  27.7 4.4 %collective-permute-start.10 = (bf16[4,2,32,512]{3,2,1,0:T(8,128)(2,1)S(1)}, bf16[4,2,32,512]{3,2,1,0:T(8,128)(2,1)S(1)}, u32[]{:S(2)}, u32[]{:S(2)}) collective-permute-start(bf16[4,2,32,512]{3,2,1,0:T(8,128)(2,1)S(1)} %collective-permute-done.9), channel_id=1, source_target_pairs={{1,0},{2,1},{3,2},{4,3},{5,4},{6,5},{7,6},{8,7},{9,8},{10,9},{11,1... | collective-permute-start | bytes 786440 | tf_op jit(solution)/shard_map/ppermute | solution.py:56
  32.1 3.4 %collective-permute-done.3 = bf16[4,2,32,512]{3,2,1,0:T(8,128)(2,1)S(1)} collective-permute-done((bf16[4,2,32,512]{3,2,1,0:T(8,128)(2,1)S(1)}, bf16[4,2,32,512]{3,2,1,0:T(8,128)(2,1)S(1)}, u32[]{:S(2)}, u32[]{:S(2)}) %collective-permute-start.3) | collective-permute-done | bytes 262176 | tf_op jit(solution)/shard_map/ppermute | solution.py:54
  35.5 0.1 convert_reduce_fusion
  35.6 0.8 copy.47
  36.3 0.8 copy.48
  37.1 0.7 iota_compare_fusion.5
  37.8 4.4 %collective-permute-start.11 = (bf16[4,2,32,512]{3,2,1,0:T(8,128)(2,1)S(1)}, bf16[4,2,32,512]{3,2,1,0:T(8,128)(2,1)S(1)}, u32[]{:S(2)}, u32[]{:S(2)}) collective-permute-start(bf16[4,2,32,512]{3,2,1,0:T(8,128)(2,1)S(1)} %collective-permute-done.10), channel_id=1, source_target_pairs={{1,0},{2,1},{3,2},{4,3},{5,4},{6,5},{7,6},{8,7},{9,8},{10,9},{11,1... | collective-permute-start | bytes 786440 | tf_op jit(solution)/shard_map/ppermute | solution.py:56
  42.3 1.8 collective-permute-done.4
  44.1 0.2 fusion.32
  44.3 1.9 collective-permute-done.11
  46.2 4.7 %collective-permute-start.12 = (bf16[4,2,32,512]{3,2,1,0:T(8,128)(2,1)S(1)}, bf16[4,2,32,512]{3,2,1,0:T(8,128)(2,1)}, u32[]{:S(2)}, u32[]{:S(2)}) collective-permute-start(bf16[4,2,32,512]{3,2,1,0:T(8,128)(2,1)S(1)} %collective-permute-done.11), channel_id=1, source_target_pairs={{1,0},{2,1},{3,2},{4,3},{5,4},{6,5},{7,6},{8,7},{9,8},{10,9},{11,1... | collective-permute-start | bytes 786440 | tf_op jit(solution)/shard_map/ppermute | solution.py:56
  50.9 1.8 collective-permute-done.5
  52.7 1.4 fusion.22
  54.1 0.6 collective-permute-done.12
  54.8 4.8 %collective-permute-start.13 = (bf16[4,2,32,512]{3,2,1,0:T(8,128)(2,1)}, bf16[4,2,32,512]{3,2,1,0:T(8,128)(2,1)}, u32[]{:S(2)}, u32[]{:S(2)}) collective-permute-start(bf16[4,2,32,512]{3,2,1,0:T(8,128)(2,1)} %collective-permute-done.12), channel_id=1, source_target_pairs={{1,0},{2,1},{3,2},{4,3},{5,4},{6,5},{7,6},{8,7},{9,8},{10,9},{11,1... | collective-permute-start | bytes 786440 | tf_op jit(solution)/shard_map/ppermute | solution.py:56
  59.6 1.8 collective-permute-done.6
  61.4 0.6 copy.51
  62.0 1.7 collective-permute-done.13
  63.8 4.7 %collective-permute-start.14 = (bf16[4,2,32,512]{3,2,1,0:T(8,128)(2,1)}, bf16[4,2,32,512]{3,2,1,0:T(8,128)(2,1)S(1)}, u32[]{:S(2)}, u32[]{:S(2)}) collective-permute-start(bf16[4,2,32,512]{3,2,1,0:T(8,128)(2,1)} %collective-permute-done.13), channel_id=1, source_target_pairs={{1,0},{2,1},{3,2},{4,3},{5,4},{6,5},{7,6},{8,7},{9,8},{10,9},{11,1... | collective-permute-start | bytes 786440 | tf_op jit(solution)/shard_map/ppermute | solution.py:56
  68.5 1.7 collective-permute-done.7
  70.2 1.7 bitcast_dynamic-update-slice_fusion.15
  71.9 1.7 bitcast_dynamic-update-slice_fusion.14
  73.5 1.7 bitcast_dynamic-update-slice_fusion.13
  75.2 1.7 bitcast_dynamic-update-slice_fusion.12
  76.8 0.7 bitcast_dynamic-update-slice_fusion.11
  77.6 0.7 bitcast_dynamic-update-slice_fusion.10
  78.3 0.7 bitcast_dynamic-update-slice_fusion.9
  79.0 0.7 bitcast_dynamic-update-slice_fusion.8
  79.8 0.7 bitcast_dynamic-update-slice_fusion.7
  80.5 0.7 bitcast_dynamic-update-slice_fusion.6
  81.2 0.7 bitcast_dynamic-update-slice_fusion.5
  82.0 0.7 bitcast_dynamic-update-slice_fusion.4
  82.7 0.7 bitcast_dynamic-update-slice_fusion.3
  83.4 1.7 bitcast_dynamic-update-slice_fusion.2
  85.1 1.7 bitcast_dynamic-update-slice_fusion.1
  86.8 0.7 bitcast_dynamic-update-slice_fusion
  87.5 5.0 %gather_fusion = bf16[16,4,2,32,512]{4,3,2,1,0:T(8,128)(2,1)} fusion(bf16[16,4,2,32,512]{4,3,2,1,0:T(8,128)(2,1)} %bitcast_dynamic-update-slice_fusion, s32[1024]{0:T(1024)S(1)} %pad_clamp_fusion), kind=kCustom, calls=%fused_computation | custom fusion | bytes 8388672 | tf_op jit(solution)/shard_map/gather | solution.py:59
  92.5 2.7 %copy.52 = bf16[4,2,16,32,512]{4,3,2,0,1:T(8,128)(2,1)S(1)} copy(bf16[4,2,16,32,512]{4,3,1,0,2:T(8,128)(2,1)} %bitcast.101) | data formatting | bytes 8388608 | tf_op jit(solution)/shard_map/transpose | solution.py:12
  95.1 0.3 slice_bitcast_fusion
  95.4 0.1 fusion.65
  95.5 1.3 fusion.29
  96.8 1.6 convolution_convert_fusion
  98.4 4.3 %copy.54 = bf16[16,8,16,1024]{3,2,1,0:T(8,128)(2,1)} copy(bf16[16,8,16,1024]{3,0,2,1:T(8,128)(2,1)S(1)} %convolution_convert_fusion) | data formatting | bytes 8388608 | tf_op jit(solution)/shard_map/convert_element_type | solution.py:85
  102.7 4.8 %all-to-all-start = ((bf16[16,8,16,1024]{3,2,1,0:T(8,128)(2,1)}), bf16[16,8,16,1024]{3,2,1,0:T(8,128)(2,1)}, u32[]{:S(2)}, u32[]{:S(2)}) async-start(bf16[16,8,16,1024]{3,2,1,0:T(8,128)(2,1)} %copy.54), calls=%async_computation | async-start | bytes 8388608 | tf_op jit(solution)/shard_map/all_to_all | solution.py:90
  107.6 0.1 copy.68
  107.7 0.1 copy.67
  107.9 0.1 slice_bitcast_fusion.2
  108.0 76.9 %all-to-all-done = bf16[16,8,16,1024]{3,2,1,0:T(8,128)(2,1)} async-done(((bf16[16,8,16,1024]{3,2,1,0:T(8,128)(2,1)}), bf16[16,8,16,1024]{3,2,1,0:T(8,128)(2,1)}, u32[]{:S(2)}, u32[]{:S(2)}) %all-to-all-start) | async-done | bytes 4194336 | tf_op jit(solution)/shard_map/all_to_all | solution.py:90
  184.8 7.9 %fusion.23 = bf16[16,8,16,128]{3,2,1,0:T(8,128)(2,1)S(1)} fusion(bf16[16,8,16,1024]{3,2,1,0:T(8,128)(2,1)} %all-to-all-done, bf16[512,512]{1,0:T(8,128)(2,1)S(1)} %get-tuple-element.8, bf16[512,512]{1,0:T(8,128)(2,1)S(1)} %fusion.64, bf16[512,512]{1,0:T(8,128)(2,1)S(1)} %get-tuple-element.7, bf16[512,64]{1,0:T(8,128)(2,1)S(1)} %bitcast.105, ...), kind=kOutput, calls=%fused_computation.24 | convolution fusion | flops 4843634688 | bytes 6488064 | tf_op jit(solution)/shard_map/smrw,wv->smrv/dot_general | solution.py:94
  192.8 0.1 copy.57
  192.9 33.7 %all_to_all.10 = bf16[16,8,16,128]{3,1,2,0:T(8,128)(2,1)S(1)} all-to-all(bf16[16,8,16,128]{3,1,2,0:T(8,128)(2,1)S(1)} %copy.57), channel_id=1, replica_groups=mesh['grp'=2,'bits'=16] {'bits'}, dimensions={0} | all-to-all | bytes 1048576 | tf_op jit(solution)/shard_map/all_to_all | solution.py:97
  226.6 0.4 convolution_bitcast_fusion
  227.0 0.6 copy.59
  (25 shorter events, 0.2 us)
Async XLA Ops:
  0.0 79.8 %copy-start.1 = (bf16[4,2,32,512]{3,2,1,0:T(8,128)(2,1)S(1)}, bf16[4,2,32,512]{3,2,1,0:T(8,128)(2,1)}, u32[]{:S(2)}) copy-start(bf16[4,2,32,512]{3,2,1,0:T(8,128)(2,1)} %param.9) | copy-start | bytes 786436
  0.0 9.8 %collective-permute-start = (bf16[4,2,32,512]{3,2,1,0:T(8,128)(2,1)}, bf16[4,2,32,512]{3,2,1,0:T(8,128)(2,1)S(1)}, u32[]{:S(2)}, u32[]{:S(2)}) collective-permute-start(bf16[4,2,32,512]{3,2,1,0:T(8,128)(2,1)} %param.9), channel_id=1, source_target_pairs={{0,1},{1,2},{2,3},{3,4},{4,5},{5,6},{6,7},{7,8},{8,9},{9,10},{10,1... | collective-permute-start | bytes 786440 | tf_op jit(solution)/shard_map/ppermute | solution.py:54
  9.8 8.5 %collective-permute-start.1 = (bf16[4,2,32,512]{3,2,1,0:T(8,128)(2,1)S(1)}, bf16[4,2,32,512]{3,2,1,0:T(8,128)(2,1)S(1)}, u32[]{:S(2)}, u32[]{:S(2)}) collective-permute-start(bf16[4,2,32,512]{3,2,1,0:T(8,128)(2,1)S(1)} %collective-permute-done), channel_id=1, source_target_pairs={{0,1},{1,2},{2,3},{3,4},{4,5},{5,6},{6,7},{7,8},{8,9},{9,10},{10,1... | collective-permute-start | bytes 786440 | tf_op jit(solution)/shard_map/ppermute | solution.py:54
  9.8 8.6 %collective-permute-start.8 = (bf16[4,2,32,512]{3,2,1,0:T(8,128)(2,1)}, bf16[4,2,32,512]{3,2,1,0:T(8,128)(2,1)S(1)}, u32[]{:S(2)}, u32[]{:S(2)}) collective-permute-start(bf16[4,2,32,512]{3,2,1,0:T(8,128)(2,1)} %param.9), channel_id=1, source_target_pairs={{1,0},{2,1},{3,2},{4,3},{5,4},{6,5},{7,6},{8,7},{9,8},{10,9},{11,1... | collective-permute-start | bytes 786440 | tf_op jit(solution)/shard_map/ppermute | solution.py:56
  18.3 8.6 %collective-permute-start.2 = (bf16[4,2,32,512]{3,2,1,0:T(8,128)(2,1)S(1)}, bf16[4,2,32,512]{3,2,1,0:T(8,128)(2,1)S(1)}, u32[]{:S(2)}, u32[]{:S(2)}) collective-permute-start(bf16[4,2,32,512]{3,2,1,0:T(8,128)(2,1)S(1)} %collective-permute-done.1), channel_id=1, source_target_pairs={{0,1},{1,2},{2,3},{3,4},{4,5},{5,6},{6,7},{7,8},{8,9},{9,10},{10,1... | collective-permute-start | bytes 786440 | tf_op jit(solution)/shard_map/ppermute | solution.py:54
  18.5 9.2 %collective-permute-start.9 = (bf16[4,2,32,512]{3,2,1,0:T(8,128)(2,1)S(1)}, bf16[4,2,32,512]{3,2,1,0:T(8,128)(2,1)S(1)}, u32[]{:S(2)}, u32[]{:S(2)}) collective-permute-start(bf16[4,2,32,512]{3,2,1,0:T(8,128)(2,1)S(1)} %collective-permute-done.8), channel_id=1, source_target_pairs={{1,0},{2,1},{3,2},{4,3},{5,4},{6,5},{7,6},{8,7},{9,8},{10,9},{11,1... | collective-permute-start | bytes 786440 | tf_op jit(solution)/shard_map/ppermute | solution.py:56
  26.9 8.6 %collective-permute-start.3 = (bf16[4,2,32,512]{3,2,1,0:T(8,128)(2,1)S(1)}, bf16[4,2,32,512]{3,2,1,0:T(8,128)(2,1)S(1)}, u32[]{:S(2)}, u32[]{:S(2)}) collective-permute-start(bf16[4,2,32,512]{3,2,1,0:T(8,128)(2,1)S(1)} %collective-permute-done.2), channel_id=1, source_target_pairs={{0,1},{1,2},{2,3},{3,4},{4,5},{5,6},{6,7},{7,8},{8,9},{9,10},{10,1... | collective-permute-start | bytes 786440 | tf_op jit(solution)/shard_map/ppermute | solution.py:54
  27.7 10.2 %collective-permute-start.10 = (bf16[4,2,32,512]{3,2,1,0:T(8,128)(2,1)S(1)}, bf16[4,2,32,512]{3,2,1,0:T(8,128)(2,1)S(1)}, u32[]{:S(2)}, u32[]{:S(2)}) collective-permute-start(bf16[4,2,32,512]{3,2,1,0:T(8,128)(2,1)S(1)} %collective-permute-done.9), channel_id=1, source_target_pairs={{1,0},{2,1},{3,2},{4,3},{5,4},{6,5},{7,6},{8,7},{9,8},{10,9},{11,1... | collective-permute-start | bytes 786440 | tf_op jit(solution)/shard_map/ppermute | solution.py:56
  35.5 8.6 %collective-permute-start.4 = (bf16[4,2,32,512]{3,2,1,0:T(8,128)(2,1)S(1)}, bf16[4,2,32,512]{3,2,1,0:T(8,128)(2,1)S(1)}, u32[]{:S(2)}, u32[]{:S(2)}) collective-permute-start(bf16[4,2,32,512]{3,2,1,0:T(8,128)(2,1)S(1)} %collective-permute-done.3), channel_id=1, source_target_pairs={{0,1},{1,2},{2,3},{3,4},{4,5},{5,6},{6,7},{7,8},{8,9},{9,10},{10,1... | collective-permute-start | bytes 786440 | tf_op jit(solution)/shard_map/ppermute | solution.py:54
  37.8 8.3 %collective-permute-start.11 = (bf16[4,2,32,512]{3,2,1,0:T(8,128)(2,1)S(1)}, bf16[4,2,32,512]{3,2,1,0:T(8,128)(2,1)S(1)}, u32[]{:S(2)}, u32[]{:S(2)}) collective-permute-start(bf16[4,2,32,512]{3,2,1,0:T(8,128)(2,1)S(1)} %collective-permute-done.10), channel_id=1, source_target_pairs={{1,0},{2,1},{3,2},{4,3},{5,4},{6,5},{7,6},{8,7},{9,8},{10,9},{11,1... | collective-permute-start | bytes 786440 | tf_op jit(solution)/shard_map/ppermute | solution.py:56
  44.1 17.3 %copy-start.2 = (bf16[4,2,32,512]{3,2,1,0:T(8,128)(2,1)}, bf16[4,2,32,512]{3,2,1,0:T(8,128)(2,1)S(1)}, u32[]{:S(2)}) copy-start(bf16[4,2,32,512]{3,2,1,0:T(8,128)(2,1)S(1)} %collective-permute-done.4) | copy-start | bytes 786436
  44.1 8.6 %collective-permute-start.5 = (bf16[4,2,32,512]{3,2,1,0:T(8,128)(2,1)S(1)}, bf16[4,2,32,512]{3,2,1,0:T(8,128)(2,1)S(1)}, u32[]{:S(2)}, u32[]{:S(2)}) collective-permute-start(bf16[4,2,32,512]{3,2,1,0:T(8,128)(2,1)S(1)} %collective-permute-done.4), channel_id=1, source_target_pairs={{0,1},{1,2},{2,3},{3,4},{4,5},{5,6},{6,7},{7,8},{8,9},{9,10},{10,1... | collective-permute-start | bytes 786440 | tf_op jit(solution)/shard_map/ppermute | solution.py:54
  46.2 8.6 %collective-permute-start.12 = (bf16[4,2,32,512]{3,2,1,0:T(8,128)(2,1)S(1)}, bf16[4,2,32,512]{3,2,1,0:T(8,128)(2,1)}, u32[]{:S(2)}, u32[]{:S(2)}) collective-permute-start(bf16[4,2,32,512]{3,2,1,0:T(8,128)(2,1)S(1)} %collective-permute-done.11), channel_id=1, source_target_pairs={{1,0},{2,1},{3,2},{4,3},{5,4},{6,5},{7,6},{8,7},{9,8},{10,9},{11,1... | collective-permute-start | bytes 786440 | tf_op jit(solution)/shard_map/ppermute | solution.py:56
  52.7 8.7 %copy-start.3 = (bf16[4,2,32,512]{3,2,1,0:T(8,128)(2,1)}, bf16[4,2,32,512]{3,2,1,0:T(8,128)(2,1)S(1)}, u32[]{:S(2)}) copy-start(bf16[4,2,32,512]{3,2,1,0:T(8,128)(2,1)S(1)} %collective-permute-done.5) | copy-start | bytes 786436
  52.7 8.7 %collective-permute-start.6 = (bf16[4,2,32,512]{3,2,1,0:T(8,128)(2,1)S(1)}, bf16[4,2,32,512]{3,2,1,0:T(8,128)(2,1)}, u32[]{:S(2)}, u32[]{:S(2)}) collective-permute-start(bf16[4,2,32,512]{3,2,1,0:T(8,128)(2,1)S(1)} %collective-permute-done.5), channel_id=1, source_target_pairs={{0,1},{1,2},{2,3},{3,4},{4,5},{5,6},{6,7},{7,8},{8,9},{9,10},{10,1... | collective-permute-start | bytes 786440 | tf_op jit(solution)/shard_map/ppermute | solution.py:54
  54.8 9.0 %collective-permute-start.13 = (bf16[4,2,32,512]{3,2,1,0:T(8,128)(2,1)}, bf16[4,2,32,512]{3,2,1,0:T(8,128)(2,1)}, u32[]{:S(2)}, u32[]{:S(2)}) collective-permute-start(bf16[4,2,32,512]{3,2,1,0:T(8,128)(2,1)} %collective-permute-done.12), channel_id=1, source_target_pairs={{1,0},{2,1},{3,2},{4,3},{5,4},{6,5},{7,6},{8,7},{9,8},{10,9},{11,1... | collective-permute-start | bytes 786440 | tf_op jit(solution)/shard_map/ppermute | solution.py:56
  61.4 8.8 %collective-permute-start.7 = (bf16[4,2,32,512]{3,2,1,0:T(8,128)(2,1)}, bf16[4,2,32,512]{3,2,1,0:T(8,128)(2,1)}, u32[]{:S(2)}, u32[]{:S(2)}) collective-permute-start(bf16[4,2,32,512]{3,2,1,0:T(8,128)(2,1)} %collective-permute-done.6), channel_id=1, source_target_pairs={{0,1},{1,2},{2,3},{3,4},{4,5},{5,6},{6,7},{7,8},{8,9},{9,10},{10,1... | collective-permute-start | bytes 786440 | tf_op jit(solution)/shard_map/ppermute | solution.py:54
  63.8 23.0 %collective-permute-start.14 = (bf16[4,2,32,512]{3,2,1,0:T(8,128)(2,1)}, bf16[4,2,32,512]{3,2,1,0:T(8,128)(2,1)S(1)}, u32[]{:S(2)}, u32[]{:S(2)}) collective-permute-start(bf16[4,2,32,512]{3,2,1,0:T(8,128)(2,1)} %collective-permute-done.13), channel_id=1, source_target_pairs={{1,0},{2,1},{3,2},{4,3},{5,4},{6,5},{7,6},{8,7},{9,8},{10,9},{11,1... | collective-permute-start | bytes 786440 | tf_op jit(solution)/shard_map/ppermute | solution.py:56
  102.7 4.9 %copy-start.4 = (bf16[2,512,64]{1,2,0:T(8,128)(2,1)S(1)}, bf16[2,512,64]{1,2,0:T(8,128)(2,1)}, u32[]{:S(2)}) copy-start(bf16[2,512,64]{1,2,0:T(8,128)(2,1)} %param.15) | copy-start | bytes 393220
  102.7 5.2 %copy-start = (bf16[1,2,512,512]{3,2,1,0:T(8,128)(2,1)S(1)}, bf16[1,2,512,512]{3,2,1,0:T(8,128)(2,1)}, u32[]{:S(2)}) copy-start(bf16[1,2,512,512]{3,2,1,0:T(8,128)(2,1)} %param.13) | copy-start | bytes 3145732
  102.7 82.1 %all-to-all-start = ((bf16[16,8,16,1024]{3,2,1,0:T(8,128)(2,1)}), bf16[16,8,16,1024]{3,2,1,0:T(8,128)(2,1)}, u32[]{:S(2)}, u32[]{:S(2)}) async-start(bf16[16,8,16,1024]{3,2,1,0:T(8,128)(2,1)} %copy.54), calls=%async_computation | async-start | bytes 8388608 | tf_op jit(solution)/shard_map/all_to_all | solution.py:90
